TPU v7x, 32 devices: a whole 2x2x4 slice. The times are simulated.
32 devices in a mesh: rows: 8 (over z, y), wide: 4 (over x, core).
Axes of the slice: x: 2, y: 2, z: 4, core: 2. Of those that a mesh axis runs over, the one named last changes fastest.
Arguments:
- tokens: bfloat16 [16, 1024, 1024], P('rows', 'wide'), may hold values from -6 to 6
- doc_ids: int32 [16, 1024], P('rows'), may hold values from 0 to 5, never falling along the last dimension, each value on 1 to 512 neighbouring positions
- factor_weight: bfloat16 [1024, 800], replicated, may hold values from -0.3125 to 0.3125
- output_weight: bfloat16 [1024, 1024], replicated, may hold values from -0.5 to 0.5
- norm_one: float32 [1024], replicated, may hold values from 0.5 to 1.5
- norm_two: float32 [1024], replicated, may hold values from 0.5 to 1.5
- gate_weight: bfloat16 [1024, 2816], P(None, 'wide'), may hold values from -0.1875 to 0.1875
- up_weight: bfloat16 [1024, 2816], P(None, 'wide'), may hold values from -0.1875 to 0.1875
- down_weight: bfloat16 [2816, 1024], P('wide'), may hold values from -0.15625 to 0.15625
- cotangent: bfloat16 [16, 1024, 1024], P('rows', 'wide'), may hold values from -6 to 6
Outputs:
- output: bfloat16 [16, 1024, 1024], P('rows', 'wide')
- input_grad: bfloat16 [16, 1024, 1024], P('rows', 'wide')
- grad_factors: float32 [1024, 800], replicated
- grad_out: float32 [1024, 1024], replicated
- grad_norm_one: float32 [1024], replicated
- grad_norm_two: float32 [1024], replicated
- grad_gate: float32 [1024, 2816], P(None, 'wide')
- up_weight_gradient: float32 [1024, 2816], P(None, 'wide')
- down_weight_gradient: float32 [2816, 1024], P('wide')
Inputs may be any that keep to these rules, and one draw needn't show every extreme that they name: `doc_ids`: in each sequence the ids never fall along the positions; a document holds 1 to 512 positions, and one document of every sequence holds exactly 512.
All inputs are finite; a program needn't handle non-finite values.
Results may differ from a plain program's by a relative error of at most 0.017.
The roundings to bfloat16 on the way count: a program that leaves them out, or rounds other values in their place, can miss the bound.
Values may be sent and summed in bfloat16 or wider, within the bound.
A program may use at most 256 MiB of HBM per device.

v0:
```python
import jax
import jax.numpy as jnp
from jax import lax
from jax.sharding import PartitionSpec as P

H = 16
DH = 64
RQ = 6
RK = 2
SEQ_BLOCK = 2
EPS = 1e-06
NEG = -1000000000.0
MATMUL_EXACTNESS = lax.Precision.HIGHEST


def expand(part_a, part_b, heads, rank):
    leading = part_a.shape[:-1]
    left_part = part_a.reshape(leading + (heads, rank))
    right_part = part_b.reshape(leading + (rank, -1))
    return (
        jnp.einsum("...hr,...rd->...hd", left_part, right_part, preferred_element_type=jnp.float32)
        / rank
    )


def factor_grads(grad_heads, part_a, part_b, heads, rank):
    leading = part_a.shape[:-1]
    left_part = part_a.reshape(leading + (heads, rank)).astype(jnp.float32)
    right_part = part_b.reshape(leading + (rank, -1)).astype(jnp.float32)
    grad_left = (
        jnp.einsum("...hd,...rd->...hr", grad_heads, right_part, precision=MATMUL_EXACTNESS) / rank
    )
    grad_right = (
        jnp.einsum("...hd,...hr->...rd", grad_heads, left_part, precision=MATMUL_EXACTNESS) / rank
    )
    return (grad_left.reshape(leading + (-1,)), grad_right.reshape(leading + (-1,)))


def split_query(factor_rows):
    cut_one = H * RQ
    return (factor_rows[..., :cut_one], factor_rows[..., cut_one:])


def split_pair(factor_rows):
    cut_one = H * RK
    cut_two = cut_one + RK * DH
    cut_three = cut_two + H * RK
    return (
        factor_rows[..., :cut_one],
        factor_rows[..., cut_one:cut_two],
        factor_rows[..., cut_two:cut_three],
        factor_rows[..., cut_three:],
    )


def block_scores(queries, key_heads, allowed):
    scores = jnp.einsum(
        "sqhd,skhd->shqk", queries, key_heads, preferred_element_type=jnp.float32
    ) * DH ** (-0.5)
    return jnp.where(allowed[:, None], scores, NEG)


def attend_forward(block_parts):
    queries, key_heads, value_heads, allowed = block_parts
    scores = block_scores(queries, key_heads, allowed)
    row_top = jnp.max(scores, axis=-1, keepdims=True)
    exponent = jnp.exp(scores - row_top)
    totals = jnp.sum(exponent, axis=-1, keepdims=True)
    attn_probs = (exponent / totals).astype(jnp.bfloat16)
    mixed_out = jnp.einsum(
        "shqk,skhd->sqhd", attn_probs, value_heads, preferred_element_type=jnp.float32
    )
    return (mixed_out.astype(jnp.bfloat16), (row_top + jnp.log(totals))[..., 0])


def attend_backward(block_parts):
    queries, key_heads, value_heads, allowed, logsum, grad_mixed = block_parts
    scores = block_scores(queries, key_heads, allowed)
    attn_probs = jnp.exp(scores - logsum[..., None])
    grad_probs = jnp.einsum(
        "sqhd,skhd->shqk", grad_mixed, value_heads, preferred_element_type=jnp.float32
    )
    inner_sum = jnp.sum(attn_probs * grad_probs, axis=-1, keepdims=True)
    grad_scores = (attn_probs * (grad_probs - inner_sum)).astype(jnp.bfloat16)
    scaling = DH ** (-0.5)
    grad_query = (
        jnp.einsum("shqk,skhd->sqhd", grad_scores, key_heads, preferred_element_type=jnp.float32)
        * scaling
    )
    grad_key = (
        jnp.einsum("shqk,sqhd->skhd", grad_scores, queries, preferred_element_type=jnp.float32)
        * scaling
    )
    grad_value = jnp.einsum(
        "shqk,sqhd->skhd",
        attn_probs.astype(jnp.bfloat16),
        grad_mixed,
        preferred_element_type=jnp.float32,
    )
    return (grad_query, grad_key, grad_value)


def grouped(array_in):
    return array_in.reshape((array_in.shape[0] // SEQ_BLOCK, SEQ_BLOCK) + array_in.shape[1:])


def ungrouped(array_in):
    return array_in.reshape((array_in.shape[0] * array_in.shape[1],) + array_in.shape[2:])


def norm_backward(grad_normed, values, scaling, gain):
    weighted = grad_normed * gain
    grad_values = scaling * weighted - values * (scaling * scaling * scaling) * jnp.mean(
        weighted * values, axis=-1, keepdims=True
    )
    grad_gain = jnp.sum(grad_normed * values * scaling, axis=(0, 1))
    return (grad_values, grad_gain)


def body(
    tokens,
    doc_ids,
    factor_weight,
    output_weight,
    norm_one,
    norm_two,
    gate_weight,
    up_weight,
    down_weight,
    cotangent,
):
    seq_count, own_len, _unused = tokens.shape
    full_len = doc_ids.shape[1]
    offset = lax.axis_index("wide") * own_len
    query_columns = H * RQ + RQ * DH
    hidden_in = tokens.astype(jnp.float32)
    scale_one = lax.rsqrt(jnp.mean(hidden_in * hidden_in, axis=-1, keepdims=True) + EPS)
    first_normalized = (hidden_in * scale_one * norm_one).astype(jnp.bfloat16)
    normalized_total = lax.all_gather(first_normalized, "wide", axis=1, tiled=True)
    query_fac = jnp.einsum(
        "cnx,xo->cno",
        first_normalized,
        factor_weight[:, :query_columns],
        preferred_element_type=jnp.float32,
    ).astype(jnp.bfloat16)
    pair_fac = jnp.einsum(
        "cnx,xo->cno",
        normalized_total,
        factor_weight[:, query_columns:],
        preferred_element_type=jnp.float32,
    ).astype(jnp.bfloat16)
    query_a, query_b = split_query(query_fac)
    key_a, key_b, value_a, value_b = split_pair(pair_fac)
    queries = expand(query_a, query_b, H, RQ).astype(jnp.bfloat16)
    key_heads = expand(key_a, key_b, H, RK).astype(jnp.bfloat16)
    value_heads = expand(value_a, value_b, H, RK).astype(jnp.bfloat16)
    doc_query = lax.dynamic_slice_in_dim(doc_ids, offset, own_len, 1)
    key_pos = lax.broadcasted_iota(jnp.int32, (own_len, full_len), 1)
    query_pos = lax.broadcasted_iota(jnp.int32, (own_len, full_len), 0) + offset
    allowed = (doc_query[:, :, None] == doc_ids[:, None, :]) & (key_pos <= query_pos)[None]
    mixed_out, logsum = lax.map(
        attend_forward,
        (grouped(queries), grouped(key_heads), grouped(value_heads), grouped(allowed)),
    )
    attention_result = ungrouped(mixed_out).reshape(seq_count, own_len, H * DH)
    logsum = ungrouped(logsum)
    residual_branch = jnp.einsum(
        "trq,qx->trx", attention_result, output_weight, preferred_element_type=jnp.float32
    )
    hidden_middle = hidden_in + residual_branch
    scale_two = lax.rsqrt(jnp.mean(hidden_middle * hidden_middle, axis=-1, keepdims=True) + EPS)
    second_normalized = (hidden_middle * scale_two * norm_two).astype(jnp.bfloat16)
    input_rows_total = lax.all_gather(second_normalized, "wide", axis=1, tiled=True)
    gate_logits = jnp.einsum(
        "cnx,xo->cno", input_rows_total, gate_weight, preferred_element_type=jnp.float32
    )
    up_activation = jnp.einsum(
        "cnx,xo->cno", input_rows_total, up_weight, preferred_element_type=jnp.float32
    )
    gate_sig = jax.nn.sigmoid(gate_logits)
    feedforward_hidden = (gate_logits * gate_sig * up_activation).astype(jnp.bfloat16)
    partial_output = jnp.einsum(
        "gxk,km->gxm", feedforward_hidden, down_weight, preferred_element_type=jnp.float32
    )
    feed_out = lax.psum_scatter(
        partial_output.astype(jnp.bfloat16), "wide", scatter_dimension=1, tiled=True
    ).astype(jnp.float32)
    gradient_total = lax.all_gather(cotangent, "wide", axis=1, tiled=True)
    hidden_gradient = jnp.einsum(
        "uow,nw->uon", gradient_total, down_weight, preferred_element_type=jnp.float32
    )
    gate_logits_gradient = (
        hidden_gradient * up_activation * gate_sig * (1.0 + gate_logits * (1.0 - gate_sig))
    ).astype(jnp.bfloat16)
    up_logits_gradient = (hidden_gradient * gate_logits * gate_sig).astype(jnp.bfloat16)
    grad_in_part = jnp.einsum(
        "hnc,uc->hnu", gate_logits_gradient, gate_weight, preferred_element_type=jnp.float32
    )
    grad_in_part = grad_in_part + jnp.einsum(
        "hnc,uc->hnu", up_logits_gradient, up_weight, preferred_element_type=jnp.float32
    )
    grad_normed_two = lax.psum_scatter(
        grad_in_part.astype(jnp.bfloat16), "wide", scatter_dimension=1, tiled=True
    ).astype(jnp.float32)
    grad_gate = jnp.einsum(
        "wvm,wvu->mu", input_rows_total, gate_logits_gradient, preferred_element_type=jnp.float32
    )
    up_weight_gradient = jnp.einsum(
        "wvm,wvu->mu", input_rows_total, up_logits_gradient, preferred_element_type=jnp.float32
    )
    down_weight_gradient = jnp.einsum(
        "qmw,qmv->wv", feedforward_hidden, gradient_total, preferred_element_type=jnp.float32
    )
    grad_gate, up_weight_gradient, down_weight_gradient = (
        lax.psum(grad_gate.astype(jnp.bfloat16), "rows").astype(jnp.float32),
        lax.psum(up_weight_gradient.astype(jnp.bfloat16), "rows").astype(jnp.float32),
        lax.psum(down_weight_gradient.astype(jnp.bfloat16), "rows").astype(jnp.float32),
    )
    output = (hidden_middle + feed_out).astype(jnp.bfloat16)
    grad_mid_norm, gain_two = norm_backward(grad_normed_two, hidden_middle, scale_two, norm_two)
    grad_mid = cotangent.astype(jnp.float32) + grad_mid_norm
    branch_gradient = grad_mid.astype(jnp.bfloat16)
    grad_w_out = jnp.einsum(
        "amx,amb->xb", attention_result, branch_gradient, preferred_element_type=jnp.float32
    )
    grad_attended = jnp.einsum(
        "pjk,zk->pjz", branch_gradient, output_weight, preferred_element_type=jnp.float32
    ).astype(jnp.bfloat16)
    grad_attended = grad_attended.reshape(seq_count, own_len, H, DH)
    grad_query, grad_key, grad_value = lax.map(
        attend_backward,
        (
            grouped(queries),
            grouped(key_heads),
            grouped(value_heads),
            grouped(allowed),
            grouped(logsum),
            grouped(grad_attended),
        ),
    )
    grad_query = ungrouped(grad_query)
    grad_key = ungrouped(grad_key)
    grad_value = ungrouped(grad_value)
    grad_qa, grad_qb = factor_grads(grad_query, query_a, query_b, H, RQ)
    grad_ka, grad_kb = factor_grads(grad_key, key_a, key_b, H, RK)
    grad_va, grad_vb = factor_grads(grad_value, value_a, value_b, H, RK)
    pair_grads = jnp.concatenate([grad_ka, grad_kb, grad_va, grad_vb], axis=-1)
    pair_own = lax.psum_scatter(
        pair_grads.astype(jnp.bfloat16), "wide", scatter_dimension=1, tiled=True
    ).astype(jnp.float32)
    factor_gradient = jnp.concatenate([grad_qa, grad_qb, pair_own], axis=-1).astype(jnp.bfloat16)
    grad_w_factors = jnp.einsum(
        "wvm,wvu->mu", first_normalized, factor_gradient, preferred_element_type=jnp.float32
    )
    grad_normed_one = jnp.einsum(
        "hnc,uc->hnu", factor_gradient, factor_weight, preferred_element_type=jnp.float32
    )
    grad_in_norm, gain_one = norm_backward(grad_normed_one, hidden_in, scale_one, norm_one)
    input_grad = (grad_mid + grad_in_norm).astype(jnp.bfloat16)
    grad_w_factors, grad_w_out, gain_one, gain_two = lax.psum(
        (grad_w_factors, grad_w_out, gain_one, gain_two), ("rows", "wide")
    )
    return (
        output,
        input_grad,
        grad_w_factors,
        grad_w_out,
        gain_one,
        gain_two,
        grad_gate,
        up_weight_gradient,
        down_weight_gradient,
    )


def solution(mesh):
    placed = (
        P("rows", "wide", None),
        P("rows", None),
        P(),
        P(),
        P(),
        P(),
        P(None, "wide"),
        P(None, "wide"),
        P("wide", None),
        P("rows", "wide", None),
    )
    return jax.shard_map(
        body,
        mesh=mesh,
        in_specs=placed,
        out_specs=(
            P("rows", "wide", None),
            P("rows", "wide", None),
            P(),
            P(),
            P(),
            P(),
            P(None, "wide"),
            P(None, "wide"),
            P("wide", None),
        ),
        check_vma=False,
    )
```

profile of v0, /device:TPU:0, one launch (start us, length us, event | category | flops | bytes accessed | tf_op | source)
XLA Modules:
  0.0 899.3 jit_solution(4847978893055860476)
XLA Ops:
  7.2 1.6 fusion.16
  10.1 2.5 fusion.18
  12.6 2.2 convolution_convert_fusion.2
  17.2 1.5 copy.89
  18.7 4.1 fusion.67
  22.8 5.3 copy.91
  29.6 20.3 %all-gather.4.cloned.1.call-done = bf16[2,1024,1024]{2,1,0:T(8,128)(2,1)} async-done(((bf16[2,256,1024]{2,1,0:T(8,128)(2,1)}), bf16[2,1024,1024]{2,1,0:T(8,128)(2,1)}) %all-gather.4.cloned.1.call-update) | async-done | bytes 4194320 | tf_op jit(solution)/shard_map/all_gather | solution.py:139
  49.9 3.9 convolution_convert_fusion.1
  54.9 2.4 copy.93
  57.3 2.1 copy.92
  59.4 7.8 fusion.68
  67.3 12.8 %copy.94 = f32[2,1024,16,64]{1,3,2,0:T(8,128)} copy(f32[2,1024,16,64]{3,2,1,0:T(8,128)} %fusion.68) | data formatting | bytes 16777216 | tf_op jit(solution)/shard_map/...hr,...rd->...hd/dot_general | solution.py:21
  80.1 2.4 copy.86
  82.5 2.1 copy.85
  84.6 7.8 fusion.66
  92.5 12.8 %copy.87 = f32[2,1024,16,64]{1,3,2,0:T(8,128)} copy(f32[2,1024,16,64]{3,2,1,0:T(8,128)} %fusion.66) | data formatting | bytes 16777216 | tf_op jit(solution)/shard_map/...hr,...rd->...hd/dot_general | solution.py:21
  105.3 17.1 %fusion.65 = (f32[2,16,256]{2,1,0:T(8,128)S(1)}, f32[2,16,256,1024]{3,2,1,0:T(8,128)}) fusion(f32[2,1024,16,64]{1,3,2,0:T(8,128)} %copy.94, f32[2,256,16,64]{1,3,2,0:T(8,128)} %copy.91, pred[2,256,1024]{2,1,0:T(8,128)(4,1)} %compare_and_fusion), kind=kOutput, calls=%fused_computation.112 | convolution fusion | flops 1104142336 | bytes 44597248 | tf_op jit(solution)/shard_map/while/body/eval_jaxpr/sqhd,skhd->shqk/dot_general | solution.py:57
  122.4 14.7 %fusion = f32[2,16,256]{2,1,0:T(8,128)S(1)} fusion(f32[2,16,256,1024]{3,2,1,0:T(8,128)} %get-tuple-element.85, f32[2,16,256]{2,1,0:T(8,128)S(1)} %get-tuple-element.84), kind=kLoop, calls=%fused_computation.6 | loop fusion | flops 16769024 | bytes 33619968 | tf_op jit(solution)/shard_map/while/body/eval_jaxpr/reduce_sum | solution.py:68
  137.1 13.2 %fusion.38 = bf16[2,16,64,256]{3,2,1,0:T(8,128)(2,1)S(1)} fusion(f32[2,16,256,1024]{3,2,1,0:T(8,128)} %get-tuple-element.85, f32[2,16,256]{2,1,0:T(8,128)S(1)} %fusion, f32[2,16,256]{2,1,0:T(8,128)S(1)} %get-tuple-element.84, f32[2,1024,16,64]{1,3,2,0:T(8,128)S(1)} %copy-done.4), kind=kOutput, calls=%fused_computation.67 | convolution fusion | flops 1103626240 | bytes 43057152 | tf_op jit(solution)/shard_map/while/body/eval_jaxpr/shqk,skhd->sqhd/dot_general | solution.py:70
  155.1 33.8 %all-gather.6.cloned.1.call-done = bf16[2,1024,1024]{2,1,0:T(8,128)(2,1)} async-done(((bf16[2,256,1024]{2,1,0:T(8,128)(2,1)}), bf16[2,1024,1024]{2,1,0:T(8,128)(2,1)}) %all-gather.6.cloned.1.call-update) | async-done | bytes 4194320 | tf_op jit(solution)/shard_map/all_gather | solution.py:173
  188.9 8.4 fusion.43
  197.3 5.0 fusion.47
  202.4 22.6 %all-gather.8.cloned.1.call-done = bf16[2,1024,1024]{2,1,0:T(8,128)(2,1)} async-done(((bf16[2,256,1024]{2,1,0:T(8,128)(2,1)}), bf16[2,1024,1024]{2,1,0:T(8,128)(2,1)}) %all-gather.8.cloned.1.call-update) | async-done | bytes 4194320 | tf_op jit(solution)/shard_map/all_gather | solution.py:188
  225.0 10.3 %multiply_convert_fusion.3 = (bf16[2,1024,704]{1,2,0:T(8,128)(2,1)S(1)}, bf16[2,1024,704]{1,2,0:T(8,128)(2,1)S(1)}, bf16[2,1024,704]{1,2,0:T(8,128)(2,1)}) fusion(f32[2,1024,704]{1,2,0:T(8,128)} %fusion.47, f32[2,1024,704]{1,2,0:T(8,128)} %fusion.43, bf16[2,1024,1024]{2,1,0:T(8,128)(2,1)} %all-gather.8.cloned.1.call-done, bf16[704,1024]{1,0:T(8,128)(2,1)} %param.18), kind=kOutput, calls=%fused_computation.15 | convolution fusion | flops 2975858688 | bytes 25821184 | tf_op jit(solution)/shard_map/uow,nw->uon/dot_general | solution.py:189
  235.3 3.5 fusion.45
  238.9 5.1 add_convert_fusion
  244.2 7.8 convolution_convert_fusion
  252.1 36.6 %reduce-scatter.6.cloned.1.call-done = bf16[2,256,1024]{2,1,0:T(8,128)(2,1)} async-done(((bf16[2,1024,1024]{2,1,0:T(8,128)(2,1)}), bf16[2,256,1024]{2,1,0:T(8,128)(2,1)}) %reduce-scatter.6.cloned.1.call-update) | async-done | bytes 1048592 | tf_op jit(solution)/shard_map/reduce_scatter | solution.py:202
  288.7 3.1 fusion.15
  291.9 43.8 %reduce-scatter.4.cloned.1.call-done = bf16[2,256,1024]{2,1,0:T(8,128)(2,1)} async-done(((bf16[2,1024,1024]{2,1,0:T(8,128)(2,1)}), bf16[2,256,1024]{2,1,0:T(8,128)(2,1)}) %reduce-scatter.4.cloned.1.call-update) | async-done | bytes 1048592 | tf_op jit(solution)/shard_map/reduce_scatter | solution.py:185
  335.7 3.9 fusion.12
  343.1 25.8 %multiply_reduce_fusion = (f32[2,16,256]{2,1,0:T(8,128)S(1)}, f32[2,16,256,1024]{3,2,1,0:T(8,128)}) fusion(f32[2,16,256,1024]{3,2,1,0:T(8,128)} %get-tuple-element.85, f32[2,16,256]{2,1,0:T(8,128)S(1)} %log_add_fusion, bf16[2,256,16,64]{1,3,2,0:T(8,128)(2,1)S(1)} %bitcast.112, f32[2,1024,16,64]{1,3,2,0:T(8,128)} %copy.87), kind=kOutput, calls=%fused_computation.1 | convolution fusion | flops 1103093760 | bytes 76611584 | tf_op jit(solution)/shard_map/while/body/eval_jaxpr/sqhd,skhd->shqk/dot_general | solution.py:80
  368.9 27.9 %multiply_convert_fusion = bf16[2,16,256,1024]{3,2,1,0:T(8,128)(2,1)} fusion(f32[2,16,256,1024]{3,2,1,0:T(8,128)} %get-tuple-element.89, f32[2,16,256,1024]{3,2,1,0:T(8,128)} %get-tuple-element.85, f32[2,16,256]{2,1,0:T(8,128)S(1)} %get-tuple-element.88, f32[2,16,256]{2,1,0:T(8,128)S(1)} %log_add_fusion), kind=kLoop, calls=%fused_computation | loop fusion | flops 33554432 | bytes 83951616 | tf_op jit(solution)/shard_map/while/body/eval_jaxpr/convert_element_type | solution.py:84
  396.8 12.0 %multiply_bitcast_fusion = f32[2,1024,16,64]{1,3,2,0:T(8,128)} fusion(bf16[2,16,256,1024]{3,2,1,0:T(8,128)(2,1)} %multiply_convert_fusion, f32[2,256,16,64]{1,3,2,0:T(8,128)S(1)} %copy-done.6), kind=kOutput, calls=%fused_computation.11 | convolution fusion | flops 1076887552 | bytes 27262976 | tf_op jit(solution)/shard_map/while/body/eval_jaxpr/shqk,sqhd->skhd/dot_general | solution.py:91
  408.9 14.6 %copy.104 = f32[2,1024,16,64]{3,2,1,0:T(8,128)} copy(f32[2,1024,16,64]{1,3,2,0:T(8,128)} %multiply_bitcast_fusion) | data formatting | bytes 16777216 | tf_op jit(solution)/shard_map/while/body/eval_jaxpr/mul | solution.py:91
  423.5 17.1 %fusion.70 = f32[2,1024,16,2]{2,3,1,0:T(2,128)} fusion(f32[2,1024,16,64]{3,2,1,0:T(8,128)} %copy.104, bf16[2,1024,2,64]{3,2,1,0:T(2,128)(2,1)S(1)} %copy-done.14), kind=kOutput, calls=%fused_computation.117 | convolution fusion | flops 50331648 | bytes 9175040 | tf_op jit(solution)/shard_map/...hd,...rd->...hr/dot_general | solution.py:31
  440.7 9.6 %fusion.71 = f32[2,1024,2,64]{3,2,1,0:T(2,128)} fusion(bf16[2,1024,16,2]{2,3,1,0:T(2,128)(2,1)S(1)} %copy-done.15, f32[2,1024,16,64]{3,2,1,0:T(8,128)S(1)} %copy-done.2), kind=kOutput, calls=%fused_computation.118 | convolution fusion | flops 50331648 | bytes 9568256 | tf_op jit(solution)/shard_map/...hd,...hr->...rd/dot_general | solution.py:34
  450.3 16.8 %fusion.6 = f32[2,1024,16,64]{1,3,2,0:T(8,128)} fusion(bf16[2,256,16,64]{1,3,2,0:T(8,128)(2,1)S(1)} %bitcast.113, f32[2,16,256,1024]{3,2,1,0:T(8,128)} %get-tuple-element.85, f32[2,16,256]{2,1,0:T(8,128)S(1)} %log_add_fusion), kind=kOutput, calls=%fused_computation.25 | convolution fusion | flops 1090519040 | bytes 43024384 | tf_op jit(solution)/shard_map/while/body/eval_jaxpr/shqk,sqhd->skhd/dot_general | solution.py:94
  467.1 14.6 %copy.111 = f32[2,1024,16,64]{3,2,1,0:T(8,128)} copy(f32[2,1024,16,64]{1,3,2,0:T(8,128)} %fusion.6) | data formatting | bytes 16777216 | tf_op jit(solution)/shard_map/while/body/eval_jaxpr/shqk,sqhd->skhd/transpose | solution.py:94
  481.7 17.1 %fusion.72 = f32[2,1024,16,2]{2,3,1,0:T(2,128)} fusion(f32[2,1024,16,64]{3,2,1,0:T(8,128)} %copy.111, bf16[2,1024,2,64]{3,2,1,0:T(2,128)(2,1)S(1)} %copy-done.12), kind=kOutput, calls=%fused_computation.119 | convolution fusion | flops 50331648 | bytes 9175040 | tf_op jit(solution)/shard_map/...hd,...rd->...hr/dot_general | solution.py:31
  498.8 9.8 %fusion.73 = f32[2,1024,2,64]{3,2,1,0:T(2,128)} fusion(bf16[2,1024,16,2]{2,3,1,0:T(2,128)(2,1)S(1)} %copy-done.16, f32[2,1024,16,64]{3,2,1,0:T(8,128)S(1)} %copy-done.3), kind=kOutput, calls=%fused_computation.120 | convolution fusion | flops 50331648 | bytes 9568256 | tf_op jit(solution)/shard_map/...hd,...hr->...rd/dot_general | solution.py:34
  508.6 2.8 copy.106
  513.4 2.6 copy.113
  517.3 2.2 pad_maximum_fusion
  519.6 7.6 bitcast_convert_fusion.1
  527.2 4.2 bitcast_convert_fusion.2
  531.4 4.2 bitcast_convert_fusion
  535.7 12.4 %multiply_bitcast_fusion.1 = f32[2,256,16,64]{1,3,2,0:T(8,128)} fusion(bf16[2,16,256,1024]{3,2,1,0:T(8,128)(2,1)} %multiply_convert_fusion, f32[2,1024,16,64]{1,3,2,0:T(8,128)} %copy.94), kind=kOutput, calls=%fused_computation.55 | convolution fusion | flops 1078460416 | bytes 27262976 | tf_op jit(solution)/shard_map/while/body/eval_jaxpr/shqk,skhd->sqhd/dot_general | solution.py:87
  548.2 5.1 copy.97
  553.3 6.9 fusion.69
  560.1 2.1 copy.99
  563.0 4.5 multiply_convert_fusion.6
  568.1 5.0 convolution_bitcast_fusion
  573.1 3.7 convolution_bitcast_fusion.1
  576.8 133.3 %all-reduce.8.cloned.1.call-done = (bf16[1024,704]{0,1:T(8,128)(2,1)}, bf16[1024,704]{0,1:T(8,128)(2,1)}, bf16[704,1024]{1,0:T(8,128)(2,1)}) async-done(((bf16[1024,704]{0,1:T(8,128)(2,1)}, bf16[1024,704]{0,1:T(8,128)(2,1)}, bf16[704,1024]{1,0:T(8,128)(2,1)}), (bf16[1024,704]{0,1:T(8,128)(2,1)}, bf16[1024,704]{0,1:T(8,128)(2,1)}, bf16[704,1024]{1,0:T(8,128)(2,1)})) %all-reduce.8.cloned.1.call-update) | async-done | bytes 4325392 | tf_op jit(solution)/shard_map/psum | solution.py:215
  710.1 3.4 convert_element_type.132
  713.5 1.9 convert_element_type.134
  715.5 1.9 convert_element_type.136
  718.3 2.9 fusion.25
  721.2 40.9 %all-reduce = (f32[1024]{0:T(1024)}, f32[1024]{0:T(1024)}) all-reduce(f32[1024]{0:T(1024)S(1)} %get-tuple-element.52, f32[1024]{0:T(1024)S(1)} %copy-done.34), channel_id=1, replica_groups=mesh['rows'=8,'wide'=4] {'rows','wide'}, use_global_device_ids=true, to_apply=%region_13.14 | all-reduce | flops 2048 | bytes 16384 | tf_op jit(solution)/shard_map/psum | solution.py:260
  762.2 3.8 fusion.22
  765.9 120.0 %all-reduce.6.cloned.1.call-done = (f32[1024,800]{0,1:T(8,128)}, f32[1024,1024]{1,0:T(8,128)}) async-done(((f32[1024,800]{0,1:T(8,128)}, f32[1024,1024]{1,0:T(8,128)}), (f32[1024,800]{0,1:T(8,128)}, f32[1024,1024]{1,0:T(8,128)})) %all-reduce.6.cloned.1.call-update) | async-done | bytes 7471120 | tf_op jit(solution)/shard_map/psum | solution.py:260
  886.0 4.2 copy.127
  890.2 2.0 copy.128
  (152 shorter events, 20.5 us)
Async XLA Ops:
  7.2 143.2 %copy-start = (bf16[1024,1024]{1,0:T(8,128)(2,1)S(1)}, bf16[1024,1024]{1,0:T(8,128)(2,1)}, u32[]{:S(2)}) copy-start(bf16[1024,1024]{1,0:T(8,128)(2,1)} %param.13) | copy-start | bytes 6291460
  7.2 42.7 %all-gather.4.cloned.1.call-start = ((), (), s32[]{:S(2)}) async-start(), calls=%async_computation.3 | async-start | bytes 5242880 | tf_op jit(solution)/shard_map/all_gather | solution.py:139
  9.5 0.6 copy-start.32
  12.6 176.3 %all-gather.6.cloned.1.call-start = ((), (), s32[]{:S(2)}) async-start(), calls=%async_computation.4 | async-start | bytes 5242880 | tf_op jit(solution)/shard_map/all_gather | solution.py:173
  16.1 6.7 copy-start.17
  22.8 5.3 copy-start.36
  57.3 10.0 %copy-start.13 = (bf16[2,1024,2,64]{3,2,1,0:T(2,128)(2,1)}, bf16[2,1024,2,64]{3,2,1,0:T(2,128)(2,1)S(1)}, u32[]{:S(2)}) copy-start(bf16[2,1024,2,64]{3,2,1,0:T(2,128)(2,1)S(1)} %copy.93) | copy-start | bytes 1572868
  82.4 10.0 %copy-start.11 = (bf16[2,1024,2,64]{3,2,1,0:T(2,128)(2,1)}, bf16[2,1024,2,64]{3,2,1,0:T(2,128)(2,1)S(1)}, u32[]{:S(2)}) copy-start(bf16[2,1024,2,64]{3,2,1,0:T(2,128)(2,1)S(1)} %copy.86) | copy-start | bytes 1572868
  122.4 14.7 %copy-start.4 = (f32[2,1024,16,64]{1,3,2,0:T(8,128)S(1)}, f32[2,1024,16,64]{1,3,2,0:T(8,128)}, u32[]{:S(2)}) copy-start(f32[2,1024,16,64]{1,3,2,0:T(8,128)} %copy.87) | copy-start | bytes 25165828
  137.1 13.2 %copy-start.7 = (bf16[2,256,1024]{2,1,0:T(8,128)(2,1)S(1)}, bf16[2,256,1024]{2,1,0:T(8,128)(2,1)}, u32[]{:S(2)}) copy-start(bf16[2,256,1024]{2,1,0:T(8,128)(2,1)} %param.10) | copy-start | bytes 3145732
  150.3 1.4 copy-start.28
  150.4 2.7 copy-start.31
  151.8 1.3 copy-start.5
  154.3 70.7 %all-gather.8.cloned.1.call-start = ((), (), s32[]{:S(2)}) async-start(), calls=%async_computation.6 | async-start | bytes 5242880 | tf_op jit(solution)/shard_map/all_gather | solution.py:188
  155.0 133.7 %reduce-scatter.6.cloned.1.call-start = ((), (), s32[]{:S(2)}) async-start(), calls=%async_computation.7 | async-start | bytes 5242880 | tf_op jit(solution)/shard_map/reduce_scatter | solution.py:202
  188.9 8.4 copy-start.38
  188.9 8.4 copy-start.42
  225.0 10.4 %copy-start.43 = (bf16[1024,704]{0,1:T(8,128)(2,1)S(1)}, bf16[1024,704]{0,1:T(8,128)(2,1)}, u32[]{:S(2)}) copy-start(bf16[1024,704]{0,1:T(8,128)(2,1)} %param.16) | copy-start | bytes 4325380
  235.3 3.5 copy-start.48
  235.3 3.5 copy-start.46
  235.3 3.5 copy-start.44
  244.0 91.7 %reduce-scatter.4.cloned.1.call-start = ((), (), s32[]{:S(2)}) async-start(), calls=%async_computation.5 | async-start | bytes 5242880 | tf_op jit(solution)/shard_map/reduce_scatter | solution.py:185
  252.0 83.7 %copy-start.25 = (bf16[2,256,1024]{2,1,0:T(8,128)(2,1)S(1)}, bf16[2,256,1024]{2,1,0:T(8,128)(2,1)}, u32[]{:S(2)}) copy-start(bf16[2,256,1024]{2,1,0:T(8,128)(2,1)} %param.19) | copy-start | bytes 3145732
  252.0 321.1 %reduce-scatter.8.cloned.1.call-start = ((), (), s32[]{:S(2)}) async-start(), calls=%async_computation.8 | async-start | bytes 1638400 | tf_op jit(solution)/shard_map/reduce_scatter | solution.py:248
  339.6 1.3 copy-start.22
  343.1 25.8 %copy-start.9 = (bf16[2,256,1024]{1,2,0:T(8,128)(2,1)}, bf16[2,256,1024]{1,2,0:T(8,128)(2,1)S(1)}, u32[]{:S(2)}) copy-start(bf16[2,256,1024]{1,2,0:T(8,128)(2,1)S(1)} %copy.96) | copy-start | bytes 3145732
  368.9 27.9 %copy-start.6 = (f32[2,256,16,64]{1,3,2,0:T(8,128)S(1)}, f32[2,256,16,64]{1,3,2,0:T(8,128)}, u32[]{:S(2)}) copy-start(f32[2,256,16,64]{1,3,2,0:T(8,128)} %copy.91) | copy-start | bytes 6291460
  408.8 14.7 %copy-start.14 = (bf16[2,1024,2,64]{3,2,1,0:T(2,128)(2,1)S(1)}, bf16[2,1024,2,64]{3,2,1,0:T(2,128)(2,1)}, u32[]{:S(2)}) copy-start(bf16[2,1024,2,64]{3,2,1,0:T(2,128)(2,1)} %copy-done.13) | copy-start | bytes 1572868
  423.5 17.2 %copy-start.2 = (f32[2,1024,16,64]{3,2,1,0:T(8,128)S(1)}, f32[2,1024,16,64]{3,2,1,0:T(8,128)}, u32[]{:S(2)}) copy-start(f32[2,1024,16,64]{3,2,1,0:T(8,128)} %copy.104) | copy-start | bytes 25165828
  423.5 17.2 %copy-start.15 = (bf16[2,1024,16,2]{2,3,1,0:T(2,128)(2,1)S(1)}, bf16[2,1024,16,2]{2,3,1,0:T(2,128)(2,1)}, u32[]{:S(2)}) copy-start(bf16[2,1024,16,2]{2,3,1,0:T(2,128)(2,1)} %copy.92) | copy-start | bytes 393220
  440.7 9.6 %copy-start.10 = (bf16[2,256,1024]{1,2,0:T(8,128)(2,1)S(1)}, bf16[2,256,1024]{1,2,0:T(8,128)(2,1)}, u32[]{:S(2)}) copy-start(bf16[2,256,1024]{1,2,0:T(8,128)(2,1)} %copy-done.9) | copy-start | bytes 3145732
  467.1 14.6 %copy-start.12 = (bf16[2,1024,2,64]{3,2,1,0:T(2,128)(2,1)S(1)}, bf16[2,1024,2,64]{3,2,1,0:T(2,128)(2,1)}, u32[]{:S(2)}) copy-start(bf16[2,1024,2,64]{3,2,1,0:T(2,128)(2,1)} %copy-done.11) | copy-start | bytes 1572868
  481.7 17.1 %copy-start.3 = (f32[2,1024,16,64]{3,2,1,0:T(8,128)S(1)}, f32[2,1024,16,64]{3,2,1,0:T(8,128)}, u32[]{:S(2)}) copy-start(f32[2,1024,16,64]{3,2,1,0:T(8,128)} %copy.111) | copy-start | bytes 25165828
  481.7 17.1 %copy-start.16 = (bf16[2,1024,16,2]{2,3,1,0:T(2,128)(2,1)S(1)}, bf16[2,1024,16,2]{2,3,1,0:T(2,128)(2,1)}, u32[]{:S(2)}) copy-start(bf16[2,1024,16,2]{2,3,1,0:T(2,128)(2,1)} %copy.85) | copy-start | bytes 393220
  508.6 3.0 copy-start.21
  512.5 3.7 copy-start.20
  519.6 190.5 %all-reduce.8.cloned.1.call-start = ((), (), s32[]{:S(2)}) async-start(), calls=%async_computation.10 | async-start | bytes 8650752 | tf_op jit(solution)/shard_map/psum | solution.py:215
  519.6 7.6 copy-start.39
  519.6 7.6 copy-start.49
  527.2 4.2 copy-start.40
  527.2 4.2 copy-start.47
  535.7 350.3 %all-reduce.6.cloned.1.call-start = ((), (), s32[]{:S(2)}) async-start(), calls=%async_computation.9 | async-start | bytes 14942208 | tf_op jit(solution)/shard_map/psum | solution.py:260
  548.1 5.1 copy-start.18
  560.1 2.9 copy-start.19
  563.0 5.0 copy-start.29
  568.1 5.0 copy-start.23
  568.1 5.0 copy-start.30
  710.1 3.4 copy-start.27
  713.5 2.0 copy-start.26
  715.5 2.0 copy-start.8
  715.5 2.0 copy-start.33
  715.5 2.0 copy-start.35
  715.5 2.8 copy-start.41
  715.5 2.8 copy-start.45
  718.3 2.9 copy-start.34
  718.3 43.8 %copy-start.37 = (f32[2,256]{1,0:T(2,128)S(1)}, f32[2,256]{1,0:T(2,128)}, u32[]{:S(2)}) copy-start(f32[2,256]{1,0:T(2,128)} %get-tuple-element.80) | copy-start | bytes 6148
  886.0 4.2 copy-start.24
  886.0 6.2 copy-start.1
Sparse Core Ops, SparseCore 0:
  12.7 37.1 all-gather.3
  154.4 34.4 all-gather.5
  190.5 34.4 all-gather.7
  244.1 44.5 reduce-scatter.5
  291.1 44.5 reduce-scatter.3
  519.7 26.4 reduce-scatter.7
  550.6 159.4 all-reduce.7
  716.7 169.1 all-reduce.5
where the time goes:
time: 904 us; the launch traced here: 899 us
  waiting for transfers between devices  411 us (45%)
  matrix products  259 us (29%)
  local copies, waits for them, and re-layouts  102 us (11%)
  other arithmetic  71.4 us (8%)
  blocking collectives  40.9 us (5%)
  between operations  14.9 us (2%)
    psum x1, waiting for transfers between devices, body(): lax.psum(grad_gate.astype(jnp.bfloat16), 'rows').astype(jnp.float32)  133 us
    psum x1, waiting for transfers between devices, body(): lax.psum((grad_w_factors, grad_w_out, gain_one, gain_two), ('rows', 'wide'))  120 us
    reduce_scatter x1, waiting for transfers between devices, body(): lax.psum_scatter(partial_output.astype(jnp.bfloat16), 'wide', scatter_dim...  43.8 us
    dot_general x3, matrix products, factor_grads(): jnp.einsum('...hd,...rd->...hr', grad_heads, right_part, precision=MATMUL...  41.1 us
    psum x1, blocking collectives, body(): lax.psum((grad_w_factors, grad_w_out, gain_one, gain_two), ('rows', 'wide'))  40.9 us
    reduce_scatter x1, waiting for transfers between devices, body(): lax.psum_scatter(grad_in_part.astype(jnp.bfloat16), 'wide', scatter_dimen...  36.6 us
    all_gather x1, waiting for transfers between devices, body(): lax.all_gather(second_normalized, 'wide', axis=1, tiled=True)  33.8 us
    dot_general x3, local copies, waits for them, and re-layouts, expand(): jnp.einsum('...hr,...rd->...hd', left_part, right_part, preferred_element...  31 us
  transfers between devices with their start and end apart: 8, of which 7 were waited for; matrix products, arithmetic and copies ran while one was open for 12% of the time, Pallas kernels for 0%

commit v1 on v0

--- a/solution.py
+++ b/solution.py
@@ -11,6 +11,12 @@
 EPS = 1e-06
 NEG = -1000000000.0
 MATMUL_EXACTNESS = lax.Precision.HIGHEST
+
+
+def laid_out(pieces, dim):
+    pieces = jnp.moveaxis(pieces, 0, dim)
+    dims = pieces.shape
+    return pieces.reshape(*dims[:dim], dims[dim] * dims[dim + 1], *dims[dim + 2 :])
 
 
 def expand(part_a, part_b, heads, rank):
@@ -136,7 +142,14 @@
     hidden_in = tokens.astype(jnp.float32)
     scale_one = lax.rsqrt(jnp.mean(hidden_in * hidden_in, axis=-1, keepdims=True) + EPS)
     first_normalized = (hidden_in * scale_one * norm_one).astype(jnp.bfloat16)
-    normalized_total = lax.all_gather(first_normalized, "wide", axis=1, tiled=True)
+    peers = lax.axis_size("wide")
+    ahead = [(i, (i + 1) % peers) for i in range(peers)]
+    blocks = [first_normalized]
+    while len(blocks) < peers:
+        blocks.append(lax.ppermute(blocks[-1], "wide", ahead))
+    position = lax.axis_index("wide")
+    blocks = jnp.stack(blocks)[(position - jnp.arange(peers)) % peers]
+    normalized_total = laid_out(blocks, 1)
     query_fac = jnp.einsum(
         "cnx,xo->cno",
         first_normalized,

time: 904 us -> 924 us (1.022)
    ppermute x0 -> x3, waiting for transfers between devices: none -> 27.1 us  [body(): blocks.append(lax.ppermute(blocks[-1], 'wide', ahead))]
    all_gather x1 -> x0, waiting for transfers between devices: 20.3 us -> none  [body(): lax.all_gather(first_normalized, 'wide', axis=1, tiled=True)]
  transfers between devices with their start and end apart: 8 -> 10, of which waited for: 7 -> 9; matrix products, arithmetic and copies ran while one was open for 12% -> 12% of each run, Pallas kernels for 0% -> 0%
where the time goes in v1:
time: 924 us; the launch traced here: 919 us
  waiting for transfers between devices  420 us (45%)
  matrix products  256 us (28%)
  local copies, waits for them, and re-layouts  110 us (12%)
  other arithmetic  74.3 us (8%)
  blocking collectives  40.9 us (4%)
  between operations  14.9 us (2%)
    psum x1, waiting for transfers between devices, body(): lax.psum(grad_gate.astype(jnp.bfloat16), 'rows').astype(jnp.float32)  133 us
    psum x1, waiting for transfers between devices, body(): lax.psum((grad_w_factors, grad_w_out, gain_one, gain_two), ('rows', 'wide'))  120 us
    reduce_scatter x1, waiting for transfers between devices, body(): lax.psum_scatter(partial_output.astype(jnp.bfloat16), 'wide', scatter_dim...  43.8 us
    dot_general x3, matrix products, factor_grads(): jnp.einsum('...hd,...rd->...hr', grad_heads, right_part, precision=MATMUL...  41.1 us
    psum x1, blocking collectives, body(): lax.psum((grad_w_factors, grad_w_out, gain_one, gain_two), ('rows', 'wide'))  40.9 us
    reduce_scatter x1, waiting for transfers between devices, body(): lax.psum_scatter(grad_in_part.astype(jnp.bfloat16), 'wide', scatter_dimen...  36.4 us
    all_gather x1, waiting for transfers between devices, body(): lax.all_gather(second_normalized, 'wide', axis=1, tiled=True)  35.9 us
    dot_general x3, local copies, waits for them, and re-layouts, expand(): jnp.einsum('...hr,...rd->...hd', left_part, right_part, preferred_element...  30.2 us
  transfers between devices with their start and end apart: 10, of which 9 were waited for; matrix products, arithmetic and copies ran while one was open for 12% of the time, Pallas kernels for 0%

profile of v1, /device:TPU:0, one launch (start us, length us, event | category | flops | bytes accessed | tf_op | source)
XLA Modules:
  0.0 918.5 jit_solution(8641462877340204601)
XLA Ops:
  11.6 14.5 %collective-permute-done = bf16[2,256,1024]{2,1,0:T(8,128)(2,1)} collective-permute-done((bf16[2,256,1024]{2,1,0:T(8,128)(2,1)S(1)}, bf16[2,256,1024]{2,1,0:T(8,128)(2,1)}, u32[]{:S(2)}, u32[]{:S(2)}) %collective-permute-start) | collective-permute-done | bytes 1048608 | tf_op jit(solution)/shard_map/ppermute | solution.py:149
  30.7 4.1 fusion.69
  34.8 4.6 copy.93
  43.9 11.3 %collective-permute-done.2 = bf16[2,256,1024]{2,1,0:T(8,128)(2,1)S(1)} collective-permute-done((bf16[2,256,1024]{2,1,0:T(8,128)(2,1)}, bf16[2,256,1024]{2,1,0:T(8,128)(2,1)S(1)}, u32[]{:S(2)}, u32[]{:S(2)}) %collective-permute-start.2) | collective-permute-done | bytes 1048608 | tf_op jit(solution)/shard_map/ppermute | solution.py:149
  55.2 3.5 pad_maximum_fusion
  58.7 5.0 gather_fusion
  63.7 2.6 copy.86
  66.3 2.7 convolution_convert_fusion.1
  70.0 3.6 copy.95
  73.7 2.0 copy.94
  75.7 8.0 fusion.70
  83.6 12.8 %copy.96 = f32[2,1024,16,64]{1,3,2,0:T(8,128)} copy(f32[2,1024,16,64]{3,2,1,0:T(8,128)} %fusion.70) | data formatting | bytes 16777216 | tf_op jit(solution)/shard_map/...hr,...rd->...hd/dot_general | solution.py:27
  96.4 3.6 copy.88
  100.0 2.0 copy.87
  102.0 8.0 fusion.68
  110.0 12.8 %copy.89 = f32[2,1024,16,64]{1,3,2,0:T(8,128)} copy(f32[2,1024,16,64]{3,2,1,0:T(8,128)} %fusion.68) | data formatting | bytes 16777216 | tf_op jit(solution)/shard_map/...hr,...rd->...hd/dot_general | solution.py:27
  122.8 17.1 %fusion.67 = (f32[2,16,256]{2,1,0:T(8,128)S(1)}, f32[2,16,256,1024]{3,2,1,0:T(8,128)}) fusion(f32[2,1024,16,64]{1,3,2,0:T(8,128)} %copy.96, f32[2,256,16,64]{1,3,2,0:T(8,128)} %copy.93, pred[2,256,1024]{2,1,0:T(8,128)(4,1)} %compare_and_fusion), kind=kOutput, calls=%fused_computation.121 | convolution fusion | flops 1104142336 | bytes 44597248 | tf_op jit(solution)/shard_map/while/body/eval_jaxpr/sqhd,skhd->shqk/dot_general | solution.py:63
  139.9 14.7 %fusion = f32[2,16,256]{2,1,0:T(8,128)S(1)} fusion(f32[2,16,256,1024]{3,2,1,0:T(8,128)} %get-tuple-element.85, f32[2,16,256]{2,1,0:T(8,128)S(1)} %get-tuple-element.84), kind=kLoop, calls=%fused_computation.7 | loop fusion | flops 16769024 | bytes 33619968 | tf_op jit(solution)/shard_map/while/body/eval_jaxpr/reduce_sum | solution.py:74
  154.6 13.1 %fusion.38 = bf16[2,16,64,256]{3,2,1,0:T(8,128)(2,1)S(1)} fusion(f32[2,16,256,1024]{3,2,1,0:T(8,128)} %get-tuple-element.85, f32[2,16,256]{2,1,0:T(8,128)S(1)} %fusion, f32[2,16,256]{2,1,0:T(8,128)S(1)} %get-tuple-element.84, f32[2,1024,16,64]{1,3,2,0:T(8,128)S(1)} %copy-done.4), kind=kOutput, calls=%fused_computation.69 | convolution fusion | flops 1103626240 | bytes 43057152 | tf_op jit(solution)/shard_map/while/body/eval_jaxpr/shqk,skhd->sqhd/dot_general | solution.py:76
  172.5 35.9 %all-gather.3.cloned.1.call-done = bf16[2,1024,1024]{2,1,0:T(8,128)(2,1)} async-done(((bf16[2,256,1024]{2,1,0:T(8,128)(2,1)}), bf16[2,1024,1024]{2,1,0:T(8,128)(2,1)}) %all-gather.3.cloned.1.call-update) | async-done | bytes 4194320 | tf_op jit(solution)/shard_map/all_gather | solution.py:186
  208.4 8.4 fusion.43
  216.8 5.0 fusion.47
  221.8 22.6 %all-gather.5.cloned.1.call-done = bf16[2,1024,1024]{2,1,0:T(8,128)(2,1)} async-done(((bf16[2,256,1024]{2,1,0:T(8,128)(2,1)}), bf16[2,1024,1024]{2,1,0:T(8,128)(2,1)}) %all-gather.5.cloned.1.call-update) | async-done | bytes 4194320 | tf_op jit(solution)/shard_map/all_gather | solution.py:201
  244.4 10.3 %multiply_convert_fusion.3 = (bf16[2,1024,704]{1,2,0:T(8,128)(2,1)S(1)}, bf16[2,1024,704]{1,2,0:T(8,128)(2,1)S(1)}, bf16[2,1024,704]{1,2,0:T(8,128)(2,1)}) fusion(f32[2,1024,704]{1,2,0:T(8,128)} %fusion.47, f32[2,1024,704]{1,2,0:T(8,128)} %fusion.43, bf16[2,1024,1024]{2,1,0:T(8,128)(2,1)} %all-gather.5.cloned.1.call-done, bf16[704,1024]{1,0:T(8,128)(2,1)} %param.18), kind=kOutput, calls=%fused_computation.16 | convolution fusion | flops 2975858688 | bytes 25821184 | tf_op jit(solution)/shard_map/uow,nw->uon/dot_general | solution.py:202
  254.8 3.5 fusion.45
  258.3 5.1 add_convert_fusion
  263.9 7.8 convolution_convert_fusion
  271.8 36.4 %reduce-scatter.6.cloned.1.call-done = bf16[2,256,1024]{2,1,0:T(8,128)(2,1)} async-done(((bf16[2,1024,1024]{2,1,0:T(8,128)(2,1)}), bf16[2,256,1024]{2,1,0:T(8,128)(2,1)}) %reduce-scatter.6.cloned.1.call-update) | async-done | bytes 1048592 | tf_op jit(solution)/shard_map/reduce_scatter | solution.py:215
  308.2 3.1 fusion.15
  311.3 43.8 %reduce-scatter.4.cloned.1.call-done = bf16[2,256,1024]{2,1,0:T(8,128)(2,1)} async-done(((bf16[2,1024,1024]{2,1,0:T(8,128)(2,1)}), bf16[2,256,1024]{2,1,0:T(8,128)(2,1)}) %reduce-scatter.4.cloned.1.call-update) | async-done | bytes 1048592 | tf_op jit(solution)/shard_map/reduce_scatter | solution.py:198
  355.1 3.9 fusion.12
  362.4 25.8 %multiply_reduce_fusion = (f32[2,16,256]{2,1,0:T(8,128)S(1)}, f32[2,16,256,1024]{3,2,1,0:T(8,128)}) fusion(f32[2,16,256,1024]{3,2,1,0:T(8,128)} %get-tuple-element.85, f32[2,16,256]{2,1,0:T(8,128)S(1)} %log_add_fusion, bf16[2,256,16,64]{1,3,2,0:T(8,128)(2,1)S(1)} %bitcast.122, f32[2,1024,16,64]{1,3,2,0:T(8,128)} %copy.89), kind=kOutput, calls=%fused_computation.2 | convolution fusion | flops 1103093760 | bytes 76611584 | tf_op jit(solution)/shard_map/while/body/eval_jaxpr/sqhd,skhd->shqk/dot_general | solution.py:86
  388.2 28.0 %multiply_convert_fusion = bf16[2,16,256,1024]{3,2,1,0:T(8,128)(2,1)} fusion(f32[2,16,256,1024]{3,2,1,0:T(8,128)} %get-tuple-element.89, f32[2,16,256,1024]{3,2,1,0:T(8,128)} %get-tuple-element.85, f32[2,16,256]{2,1,0:T(8,128)S(1)} %get-tuple-element.88, f32[2,16,256]{2,1,0:T(8,128)S(1)} %log_add_fusion), kind=kLoop, calls=%fused_computation.1 | loop fusion | flops 33554432 | bytes 83951616 | tf_op jit(solution)/shard_map/while/body/eval_jaxpr/convert_element_type | solution.py:90
  416.1 12.0 %multiply_bitcast_fusion = f32[2,1024,16,64]{1,3,2,0:T(8,128)} fusion(bf16[2,16,256,1024]{3,2,1,0:T(8,128)(2,1)} %multiply_convert_fusion, f32[2,256,16,64]{1,3,2,0:T(8,128)S(1)} %copy-done.8), kind=kOutput, calls=%fused_computation.12 | convolution fusion | flops 1076887552 | bytes 27262976 | tf_op jit(solution)/shard_map/while/body/eval_jaxpr/shqk,sqhd->skhd/dot_general | solution.py:97
  428.2 14.6 %copy.106 = f32[2,1024,16,64]{3,2,1,0:T(8,128)} copy(f32[2,1024,16,64]{1,3,2,0:T(8,128)} %multiply_bitcast_fusion) | data formatting | bytes 16777216 | tf_op jit(solution)/shard_map/while/body/eval_jaxpr/mul | solution.py:97
  442.8 17.1 %fusion.72 = f32[2,1024,16,2]{2,3,1,0:T(2,128)} fusion(f32[2,1024,16,64]{3,2,1,0:T(8,128)} %copy.106, bf16[2,1024,2,64]{3,2,1,0:T(2,128)(2,1)S(1)} %copy-done.12), kind=kOutput, calls=%fused_computation.126 | convolution fusion | flops 50331648 | bytes 9175040 | tf_op jit(solution)/shard_map/...hd,...rd->...hr/dot_general | solution.py:37
  460.0 9.7 %fusion.73 = f32[2,1024,2,64]{3,2,1,0:T(2,128)} fusion(bf16[2,1024,16,2]{2,3,1,0:T(2,128)(2,1)S(1)} %copy-done.13, f32[2,1024,16,64]{3,2,1,0:T(8,128)S(1)} %copy-done.2), kind=kOutput, calls=%fused_computation.127 | convolution fusion | flops 50331648 | bytes 9568256 | tf_op jit(solution)/shard_map/...hd,...hr->...rd/dot_general | solution.py:40
  469.7 16.8 %fusion.6 = f32[2,1024,16,64]{1,3,2,0:T(8,128)} fusion(bf16[2,256,16,64]{1,3,2,0:T(8,128)(2,1)S(1)} %bitcast.123, f32[2,16,256,1024]{3,2,1,0:T(8,128)} %get-tuple-element.85, f32[2,16,256]{2,1,0:T(8,128)S(1)} %log_add_fusion), kind=kOutput, calls=%fused_computation.27 | convolution fusion | flops 1090519040 | bytes 43024384 | tf_op jit(solution)/shard_map/while/body/eval_jaxpr/shqk,sqhd->skhd/dot_general | solution.py:100
  486.4 14.6 %copy.113 = f32[2,1024,16,64]{3,2,1,0:T(8,128)} copy(f32[2,1024,16,64]{1,3,2,0:T(8,128)} %fusion.6) | data formatting | bytes 16777216 | tf_op jit(solution)/shard_map/while/body/eval_jaxpr/shqk,sqhd->skhd/transpose | solution.py:100
  501.0 17.1 %fusion.74 = f32[2,1024,16,2]{2,3,1,0:T(2,128)} fusion(f32[2,1024,16,64]{3,2,1,0:T(8,128)} %copy.113, bf16[2,1024,2,64]{3,2,1,0:T(2,128)(2,1)S(1)} %copy-done.11), kind=kOutput, calls=%fused_computation.128 | convolution fusion | flops 50331648 | bytes 9175040 | tf_op jit(solution)/shard_map/...hd,...rd->...hr/dot_general | solution.py:37
  518.1 9.9 %fusion.75 = f32[2,1024,2,64]{3,2,1,0:T(2,128)} fusion(bf16[2,1024,16,2]{2,3,1,0:T(2,128)(2,1)S(1)} %copy-done.14, f32[2,1024,16,64]{3,2,1,0:T(8,128)S(1)} %copy-done.3), kind=kOutput, calls=%fused_computation.129 | convolution fusion | flops 50331648 | bytes 9568256 | tf_op jit(solution)/shard_map/...hd,...hr->...rd/dot_general | solution.py:40
  528.0 2.8 copy.108
  532.9 2.6 copy.115
  536.8 2.2 pad_maximum_fusion.1
  539.1 7.6 bitcast_convert_fusion.1
  546.6 4.2 bitcast_convert_fusion.2
  550.9 4.2 bitcast_convert_fusion
  555.2 12.4 %multiply_bitcast_fusion.1 = f32[2,256,16,64]{1,3,2,0:T(8,128)} fusion(bf16[2,16,256,1024]{3,2,1,0:T(8,128)(2,1)} %multiply_convert_fusion, f32[2,1024,16,64]{1,3,2,0:T(8,128)} %copy.96), kind=kOutput, calls=%fused_computation.57 | convolution fusion | flops 1078460416 | bytes 27262976 | tf_op jit(solution)/shard_map/while/body/eval_jaxpr/shqk,skhd->sqhd/dot_general | solution.py:93
  567.6 5.1 copy.99
  572.7 6.9 fusion.71
  579.6 2.1 copy.101
  582.5 4.5 multiply_convert_fusion.6
  587.5 5.0 convolution_bitcast_fusion
  592.5 3.7 convolution_bitcast_fusion.1
  596.3 133.1 %all-reduce.8.cloned.1.call-done = (bf16[1024,704]{0,1:T(8,128)(2,1)}, bf16[1024,704]{0,1:T(8,128)(2,1)}, bf16[704,1024]{1,0:T(8,128)(2,1)}) async-done(((bf16[1024,704]{0,1:T(8,128)(2,1)}, bf16[1024,704]{0,1:T(8,128)(2,1)}, bf16[704,1024]{1,0:T(8,128)(2,1)}), (bf16[1024,704]{0,1:T(8,128)(2,1)}, bf16[1024,704]{0,1:T(8,128)(2,1)}, bf16[704,1024]{1,0:T(8,128)(2,1)})) %all-reduce.8.cloned.1.call-update) | async-done | bytes 4325392 | tf_op jit(solution)/shard_map/psum | solution.py:228
  729.4 3.4 convert_element_type.132
  732.8 1.9 convert_element_type.134
  734.8 1.9 convert_element_type.136
  737.6 2.9 fusion.25
  740.5 40.9 %all-reduce = (f32[1024]{0:T(1024)}, f32[1024]{0:T(1024)}) all-reduce(f32[1024]{0:T(1024)S(1)} %get-tuple-element.52, f32[1024]{0:T(1024)S(1)} %copy-done.35), channel_id=1, replica_groups=mesh['rows'=8,'wide'=4] {'rows','wide'}, use_global_device_ids=true, to_apply=%region_13.14 | all-reduce | flops 2048 | bytes 16384 | tf_op jit(solution)/shard_map/psum | solution.py:273
  781.4 3.8 fusion.22
  785.2 120.1 %all-reduce.6.cloned.1.call-done = (f32[1024,800]{0,1:T(8,128)}, f32[1024,1024]{1,0:T(8,128)}) async-done(((f32[1024,800]{0,1:T(8,128)}, f32[1024,1024]{1,0:T(8,128)}), (f32[1024,800]{0,1:T(8,128)}, f32[1024,1024]{1,0:T(8,128)})) %all-reduce.6.cloned.1.call-update) | async-done | bytes 7471120 | tf_op jit(solution)/shard_map/psum | solution.py:273
  905.3 4.2 copy.129
  909.5 2.0 copy.130
  (163 shorter events, 28.7 us)
Async XLA Ops:
  7.2 160.6 %copy-start = (bf16[1024,1024]{1,0:T(8,128)(2,1)S(1)}, bf16[1024,1024]{1,0:T(8,128)(2,1)}, u32[]{:S(2)}) copy-start(bf16[1024,1024]{1,0:T(8,128)(2,1)} %param.13) | copy-start | bytes 6291460
  7.2 201.2 %all-gather.3.cloned.1.call-start = ((), (), s32[]{:S(2)}) async-start(), calls=%async_computation.3 | async-start | bytes 5242880 | tf_op jit(solution)/shard_map/all_gather | solution.py:186
  7.2 18.9 %copy-start.41 = (bf16[1024,800]{0,1:T(8,128)(2,1)S(1)}, bf16[1024,800]{0,1:T(8,128)(2,1)}, u32[]{:S(2)}) copy-start(bf16[1024,800]{0,1:T(8,128)(2,1)} %param.12) | copy-start | bytes 4915204
  9.5 34.1 %copy-start.33 = (f32[2,256]{1,0:T(2,128)}, f32[2,256]{1,0:T(2,128)S(1)}, u32[]{:S(2)}) copy-start(f32[2,256]{1,0:T(2,128)S(1)} %get-tuple-element.81) | copy-start | bytes 6148
  11.0 15.1 %copy-start.25 = (bf16[2,256,1024]{2,1,0:T(8,128)(2,1)}, bf16[2,256,1024]{2,1,0:T(8,128)(2,1)S(1)}, u32[]{:S(2)}) copy-start(bf16[2,256,1024]{2,1,0:T(8,128)(2,1)S(1)} %fusion.18) | copy-start | bytes 3145732
  11.1 15.0 %collective-permute-start = (bf16[2,256,1024]{2,1,0:T(8,128)(2,1)S(1)}, bf16[2,256,1024]{2,1,0:T(8,128)(2,1)}, u32[]{:S(2)}, u32[]{:S(2)}) collective-permute-start(bf16[2,256,1024]{2,1,0:T(8,128)(2,1)S(1)} %fusion.18), channel_id=1, source_target_pairs={{0,1},{1,2},{2,3},{3,0},{4,5},{5,6},{6,7},{7,4},{8,9},{9,10},{10,1... | collective-permute-start | bytes 3145736 | tf_op jit(solution)/shard_map/ppermute | solution.py:149
  26.1 14.5 %collective-permute-start.1 = (bf16[2,256,1024]{2,1,0:T(8,128)(2,1)}, bf16[2,256,1024]{2,1,0:T(8,128)(2,1)}, u32[]{:S(2)}, u32[]{:S(2)}) collective-permute-start(bf16[2,256,1024]{2,1,0:T(8,128)(2,1)} %collective-permute-done), channel_id=1, source_target_pairs={{0,1},{1,2},{2,3},{3,0},{4,5},{5,6},{6,7},{7,4},{8,9},{9,10},{10,1... | collective-permute-start | bytes 3145736 | tf_op jit(solution)/shard_map/ppermute | solution.py:149
  28.1 2.6 copy-start.15
  34.8 7.3 copy-start.36
  34.8 8.8 copy-start.6
  34.8 8.8 copy-start.31
  40.6 14.6 %collective-permute-start.2 = (bf16[2,256,1024]{2,1,0:T(8,128)(2,1)}, bf16[2,256,1024]{2,1,0:T(8,128)(2,1)S(1)}, u32[]{:S(2)}, u32[]{:S(2)}) collective-permute-start(bf16[2,256,1024]{2,1,0:T(8,128)(2,1)} %collective-permute-done.1), channel_id=1, source_target_pairs={{0,1},{1,2},{2,3},{3,0},{4,5},{5,6},{6,7},{7,4},{8,9},{9,10},{10,1... | collective-permute-start | bytes 3145736 | tf_op jit(solution)/shard_map/ppermute | solution.py:149
  139.9 14.7 %copy-start.4 = (f32[2,1024,16,64]{1,3,2,0:T(8,128)S(1)}, f32[2,1024,16,64]{1,3,2,0:T(8,128)}, u32[]{:S(2)}) copy-start(f32[2,1024,16,64]{1,3,2,0:T(8,128)} %copy.89) | copy-start | bytes 25165828
  167.8 1.4 copy-start.27
  167.8 2.7 copy-start.30
  169.2 1.3 copy-start.5
  171.7 72.7 %all-gather.5.cloned.1.call-start = ((), (), s32[]{:S(2)}) async-start(), calls=%async_computation.5 | async-start | bytes 5242880 | tf_op jit(solution)/shard_map/all_gather | solution.py:201
  172.5 135.7 %reduce-scatter.6.cloned.1.call-start = ((), (), s32[]{:S(2)}) async-start(), calls=%async_computation.6 | async-start | bytes 5242880 | tf_op jit(solution)/shard_map/reduce_scatter | solution.py:215
  208.4 8.4 copy-start.38
  208.4 8.4 copy-start.43
  244.4 10.4 %copy-start.44 = (bf16[1024,704]{0,1:T(8,128)(2,1)S(1)}, bf16[1024,704]{0,1:T(8,128)(2,1)}, u32[]{:S(2)}) copy-start(bf16[1024,704]{0,1:T(8,128)(2,1)} %param.16) | copy-start | bytes 4325380
  254.8 3.5 copy-start.49
  254.8 3.5 copy-start.47
  254.8 3.5 copy-start.45
  263.4 91.7 %reduce-scatter.4.cloned.1.call-start = ((), (), s32[]{:S(2)}) async-start(), calls=%async_computation.4 | async-start | bytes 5242880 | tf_op jit(solution)/shard_map/reduce_scatter | solution.py:198
  271.7 83.5 %copy-start.22 = (bf16[2,256,1024]{2,1,0:T(8,128)(2,1)S(1)}, bf16[2,256,1024]{2,1,0:T(8,128)(2,1)}, u32[]{:S(2)}) copy-start(bf16[2,256,1024]{2,1,0:T(8,128)(2,1)} %param.19) | copy-start | bytes 3145732
  271.7 320.8 %reduce-scatter.8.cloned.1.call-start = ((), (), s32[]{:S(2)}) async-start(), calls=%async_computation.7 | async-start | bytes 1638400 | tf_op jit(solution)/shard_map/reduce_scatter | solution.py:261
  359.0 1.3 copy-start.20
  362.3 25.8 %copy-start.9 = (bf16[2,256,1024]{1,2,0:T(8,128)(2,1)}, bf16[2,256,1024]{1,2,0:T(8,128)(2,1)S(1)}, u32[]{:S(2)}) copy-start(bf16[2,256,1024]{1,2,0:T(8,128)(2,1)S(1)} %copy.98) | copy-start | bytes 3145732
  388.2 28.0 %copy-start.8 = (f32[2,256,16,64]{1,3,2,0:T(8,128)S(1)}, f32[2,256,16,64]{1,3,2,0:T(8,128)}, u32[]{:S(2)}) copy-start(f32[2,256,16,64]{1,3,2,0:T(8,128)} %copy.93) | copy-start | bytes 6291460
  428.2 14.7 %copy-start.12 = (bf16[2,1024,2,64]{3,2,1,0:T(2,128)(2,1)S(1)}, bf16[2,1024,2,64]{3,2,1,0:T(2,128)(2,1)}, u32[]{:S(2)}) copy-start(bf16[2,1024,2,64]{3,2,1,0:T(2,128)(2,1)} %copy.95) | copy-start | bytes 1572868
  442.8 17.2 %copy-start.2 = (f32[2,1024,16,64]{3,2,1,0:T(8,128)S(1)}, f32[2,1024,16,64]{3,2,1,0:T(8,128)}, u32[]{:S(2)}) copy-start(f32[2,1024,16,64]{3,2,1,0:T(8,128)} %copy.106) | copy-start | bytes 25165828
  442.8 17.2 %copy-start.13 = (bf16[2,1024,16,2]{2,3,1,0:T(2,128)(2,1)S(1)}, bf16[2,1024,16,2]{2,3,1,0:T(2,128)(2,1)}, u32[]{:S(2)}) copy-start(bf16[2,1024,16,2]{2,3,1,0:T(2,128)(2,1)} %copy.94) | copy-start | bytes 393220
  460.0 9.7 %copy-start.10 = (bf16[2,256,1024]{1,2,0:T(8,128)(2,1)S(1)}, bf16[2,256,1024]{1,2,0:T(8,128)(2,1)}, u32[]{:S(2)}) copy-start(bf16[2,256,1024]{1,2,0:T(8,128)(2,1)} %copy-done.9) | copy-start | bytes 3145732
  486.4 14.6 %copy-start.11 = (bf16[2,1024,2,64]{3,2,1,0:T(2,128)(2,1)S(1)}, bf16[2,1024,2,64]{3,2,1,0:T(2,128)(2,1)}, u32[]{:S(2)}) copy-start(bf16[2,1024,2,64]{3,2,1,0:T(2,128)(2,1)} %copy.88) | copy-start | bytes 1572868
  501.0 17.1 %copy-start.3 = (f32[2,1024,16,64]{3,2,1,0:T(8,128)S(1)}, f32[2,1024,16,64]{3,2,1,0:T(8,128)}, u32[]{:S(2)}) copy-start(f32[2,1024,16,64]{3,2,1,0:T(8,128)} %copy.113) | copy-start | bytes 25165828
  501.0 17.1 %copy-start.14 = (bf16[2,1024,16,2]{2,3,1,0:T(2,128)(2,1)S(1)}, bf16[2,1024,16,2]{2,3,1,0:T(2,128)(2,1)}, u32[]{:S(2)}) copy-start(bf16[2,1024,16,2]{2,3,1,0:T(2,128)(2,1)} %copy.87) | copy-start | bytes 393220
  528.0 3.0 copy-start.19
  532.0 3.7 copy-start.18
  539.0 190.4 %all-reduce.8.cloned.1.call-start = ((), (), s32[]{:S(2)}) async-start(), calls=%async_computation.9 | async-start | bytes 8650752 | tf_op jit(solution)/shard_map/psum | solution.py:228
  539.0 7.6 copy-start.39
  539.0 7.6 copy-start.50
  546.6 4.3 copy-start.40
  546.6 4.3 copy-start.48
  555.1 350.2 %all-reduce.6.cloned.1.call-start = ((), (), s32[]{:S(2)}) async-start(), calls=%async_computation.8 | async-start | bytes 14942208 | tf_op jit(solution)/shard_map/psum | solution.py:273
  567.6 5.1 copy-start.16
  579.6 2.9 copy-start.17
  582.5 5.0 copy-start.28
  587.5 5.0 copy-start.26
  587.5 5.0 copy-start.29
  729.4 3.4 copy-start.24
  732.8 2.0 copy-start.23
  734.7 2.0 copy-start.7
  734.8 2.0 copy-start.32
  734.8 2.0 copy-start.34
  734.8 2.8 copy-start.42
  734.8 2.8 copy-start.46
  737.6 2.9 copy-start.35
  737.6 43.8 %copy-start.37 = (f32[2,256]{1,0:T(2,128)S(1)}, f32[2,256]{1,0:T(2,128)}, u32[]{:S(2)}) copy-start(f32[2,256]{1,0:T(2,128)} %get-tuple-element.80) | copy-start | bytes 6148
  905.3 4.2 copy-start.21
  905.3 6.2 copy-start.1
Sparse Core Ops, SparseCore 0:
  171.8 36.4 all-gather.2
  209.9 34.4 all-gather.4
  263.6 44.5 reduce-scatter.5
  310.5 44.5 reduce-scatter.3
  539.1 26.4 reduce-scatter.7
  569.9 159.4 all-reduce.7
  736.0 169.1 all-reduce.5
